TPU v7x, 32 devices: a whole 2x2x4 slice. The times are simulated.
32 devices in a mesh: seq: 2 (over x), tensor: 16 (over z, y, core).
Axes of the slice: x: 2, y: 2, z: 4, core: 2. Of those that a mesh axis runs over, the one named last changes fastest.
Arguments:
- tokens: bfloat16 [512, 4096], P(('seq', 'tensor')), may hold values from -6 to 6
- lengths: int32 [6], replicated, may hold values from 1 to 256, 512 in all
- proj_zx: bfloat16 [4096, 2, 8192], P(None, None, 'tensor'), may hold values from -0.09375 to 0.09375
- proj_bc: bfloat16 [4096, 2, 1024], P(None, None, 'tensor'), may hold values from -0.09375 to 0.09375
- proj_dt: bfloat16 [4096, 128], P(None, 'tensor'), may hold values from -0.09375 to 0.09375
- conv_x: float32 [4, 8192], P(None, 'tensor'), may hold values from -3 to 3
- conv_bc: float32 [4, 2, 1024], P(None, None, 'tensor'), may hold values from -3 to 3
- bias_x: float32 [8192], P('tensor'), may hold values from -0.5 to 0.5
- bias_bc: float32 [2, 1024], P(None, 'tensor'), may hold values from -0.5 to 0.5
- dt_bias: float32 [128], P('tensor'), may hold values from -7 to -3
- decay_rate: float32 [128], P('tensor'), may hold values from 0.02 to 1
- skip_gain: float32 [128], P('tensor'), may hold values from 0.5 to 1.5
- proj_out: bfloat16 [8192, 4096], P('tensor'), may hold values from -0.0625 to 0.0625
Outputs:
- mixed: bfloat16 [512, 4096], P(('seq', 'tensor'))
- final_states: float32 [6, 128, 64, 128], P(None, 'tensor')
Inputs may be any that keep to these rules, and one draw needn't show every extreme that they name: `lengths`: the 6 requests lie back to back in the stream in this order and fill it exactly; the longest has exactly 256 tokens.
All inputs are finite; a program needn't handle non-finite values.
Results may differ from a plain program's by a relative error of at most 0.0074.
Values may be sent and summed in bfloat16 or wider, within the bound.
A program may use at most 128 MiB of HBM per device.

v0:
```python
import jax
import jax.numpy as jnp
from jax import lax
from jax.sharding import PartitionSpec as P

GROUPS = 8


def partner_2(value, axis, bit):
    mask = 2**bit
    pairs = [(source, source ^ mask) for source in range(lax.axis_size(axis))]
    return lax.ppermute(value, axis, pairs)


def passed_along(block, axis, distance):
    devices = range(lax.axis_size(axis))
    route = [(i - distance, i) for i in devices if i - distance in devices]
    return lax.ppermute(block, axis, route)


def group_columns(bc_own, tensor_index, steps_count):
    collected = bc_own
    for bit_number in range(steps_count):
        partner = partner_2(collected, "tensor", bit_number)
        upper = tensor_index // 2**bit_number % 2
        low_first = jnp.concatenate([collected, partner], axis=2)
        high_first = jnp.concatenate([partner, collected], axis=2)
        collected = jnp.where(upper == 0, low_first, high_first)
    return collected


def body(
    tokens,
    lengths,
    proj_zx,
    proj_bc,
    proj_dt,
    conv_x,
    conv_bc,
    bias_x,
    bias_bc,
    dt_bias,
    decay_rate,
    skip_gain,
    proj_out,
):
    highest = lax.Precision.HIGHEST
    tensor_size = lax.axis_size("tensor")
    rows_dev = tokens.shape[0]
    shard_len = rows_dev * tensor_size
    seq_index = lax.axis_index("seq")
    tensor_index = lax.axis_index("tensor")
    heads_dev = decay_rate.shape[0]
    width_zx = proj_zx.shape[2]
    head_size = width_zx // heads_dev
    cols_bc = proj_bc.shape[2]
    taps_count = conv_x.shape[0]
    model_width = tokens.shape[1]
    zx_flat = proj_zx.reshape(model_width, 2 * width_zx)
    bc_flat = proj_bc.reshape(model_width, 2 * cols_bc)
    piece = lax.all_gather(tokens, "tensor", axis=0, tiled=True)
    projected = jnp.concatenate(
        [
            jnp.dot(piece, zx_flat, preferred_element_type=jnp.float32),
            jnp.dot(piece, bc_flat, preferred_element_type=jnp.float32),
            jnp.dot(piece, proj_dt, preferred_element_type=jnp.float32),
        ],
        axis=1,
    )
    gate_in = projected[:, :width_zx].astype(jnp.bfloat16)
    conv_in = projected[:, width_zx : 2 * width_zx + 2 * cols_bc].astype(jnp.bfloat16)
    step_size = jax.nn.softplus(projected[:, 2 * width_zx + 2 * cols_bc :] + dt_bias[None, :])
    row_ids = jnp.arange(shard_len, dtype=jnp.int32)
    positions = seq_index * shard_len + row_ids
    bounds = jnp.cumsum(lengths)
    reached = bounds[None, :] <= positions[:, None]
    segment = jnp.sum(reached.astype(jnp.int32), axis=1)
    seg_start = jnp.max(jnp.where(reached, bounds[None, :], 0), axis=1)
    edge_rows = conv_in[shard_len - (taps_count - 1) :]
    before = passed_along(edge_rows, "seq", 1)
    extended = jnp.concatenate([before, conv_in], axis=0)
    conv_taps = jnp.concatenate([conv_x, conv_bc.reshape(taps_count, 2 * cols_bc)], axis=1)
    conv_offset = jnp.concatenate([bias_x, bias_bc.reshape(2 * cols_bc)])
    convolved = jnp.zeros((shard_len, conv_taps.shape[1]), jnp.float32) + conv_offset[None, :]
    for lag_index in range(taps_count):
        lagged = extended[
            taps_count - 1 - lag_index : taps_count - 1 - lag_index + shard_len
        ].astype(jnp.float32)
        keep_mask = (positions - lag_index >= seg_start).astype(jnp.float32)
        convolved = convolved + conv_taps[lag_index][None, :] * lagged * keep_mask[:, None]
    activated = jax.nn.silu(convolved).astype(jnp.bfloat16)
    x_conv = activated[:, :width_zx]
    bc_own = activated[:, width_zx:].reshape(shard_len, 2, cols_bc)
    per_group = tensor_size // GROUPS
    steps_count = per_group.bit_length() - 1
    bc_group = group_columns(bc_own, tensor_index, steps_count).astype(jnp.float32)
    state_in_proj = bc_group[:, 0]
    state_out_proj = bc_group[:, 1]
    x_float = x_conv.astype(jnp.float32).reshape(shard_len, heads_dev, head_size)
    log_decay = -decay_rate[None, :] * step_size
    cumulative = jnp.cumsum(log_decay, axis=0)
    cumulative_t = cumulative.T
    valid = (segment[:, None] == segment[None, :]) & (row_ids[:, None] >= row_ids[None, :])
    spread = cumulative_t[:, :, None] - cumulative_t[:, None, :]
    decay_matrix = jnp.where(valid[None], jnp.exp(jnp.where(valid[None], spread, 0.0)), 0.0)
    scores = jnp.dot(state_out_proj, state_in_proj.T, precision=highest)
    mixing = decay_matrix * scores[None] * step_size.T[:, None, :]
    y_local = jnp.einsum("hts,shp->thp", mixing, x_float, precision=highest)
    before_pos = seq_index * shard_len - 1
    seg_before = jnp.sum((bounds <= before_pos).astype(jnp.int32))
    carried = (segment == seg_before).astype(jnp.float32)
    entry_gain = jnp.exp(cumulative) * carried[:, None]
    n_seg = lengths.shape[0]
    end_rows = bounds - 1 - seq_index * shard_len
    inside = (end_rows >= 0) & (end_rows < shard_len)
    target_rows = jnp.concatenate([end_rows, jnp.full((1,), shard_len - 1, jnp.int32)])
    target_seg = jnp.concatenate([jnp.arange(n_seg, dtype=jnp.int32), segment[shard_len - 1 :]])
    target_ok = jnp.concatenate([inside, jnp.ones((1,), bool)])
    picker = (row_ids[None, :] == target_rows[:, None]).astype(jnp.float32)
    cum_end = jnp.dot(picker, cumulative, precision=highest)
    reach = (
        target_ok[:, None]
        & (row_ids[None, :] <= target_rows[:, None])
        & (segment[None, :] == target_seg[:, None])
    )
    gap_end = cum_end[:, :, None] - cumulative_t[None, :, :]
    end_weight = (
        jnp.where(reach[:, None, :], jnp.exp(jnp.where(reach[:, None, :], gap_end, 0.0)), 0.0)
        * step_size.T[None]
    )
    states = jnp.einsum("khs,shp,sn->khpn", end_weight, x_float, state_in_proj, precision=highest)
    end_local = states[:n_seg]
    shard_state = states[n_seg]
    end_gain = jnp.where((target_ok & (target_seg == seg_before))[:, None], jnp.exp(cum_end), 0.0)
    shard_gain = end_gain[n_seg]
    end_gain_seg = end_gain[:n_seg]
    gathered = (
        lax.all_gather(shard_gain[None], "seq", axis=0, tiled=True),
        lax.all_gather(shard_state[None], "seq", axis=0, tiled=True),
        lax.all_gather(end_gain_seg[None], "seq", axis=0, tiled=True),
        lax.all_gather(end_local[None], "seq", axis=0, tiled=True),
    )
    gains_all, states_all, egains_all, elocal_all = gathered

    def fold_step(carry, item):
        gain_now, state_now = item
        return (gain_now[:, None, None] * carry + state_now, carry)

    last_state, incoming = lax.scan(
        fold_step, jnp.zeros(shard_state.shape, jnp.float32), (gains_all, states_all)
    )
    state_entry = lax.dynamic_index_in_dim(incoming, seq_index, 0, keepdims=False)
    final_states = jnp.sum(elocal_all + egains_all[:, :, :, None, None] * incoming[:, None], axis=0)
    y_entry = (
        jnp.einsum("tn,hpn->thp", state_out_proj, state_entry, precision=highest)
        * entry_gain[:, :, None]
    )
    y_total = y_local + y_entry + skip_gain[None, :, None] * x_float
    gate_values = jax.nn.silu(gate_in.astype(jnp.float32)).reshape(shard_len, heads_dev, head_size)
    gated = (y_total * gate_values).reshape(shard_len, width_zx).astype(jnp.bfloat16)
    mixed = lax.psum_scatter(
        jnp.dot(gated, proj_out, preferred_element_type=jnp.float32),
        "tensor",
        scatter_dimension=0,
        tiled=True,
    )
    return (mixed.astype(jnp.bfloat16), final_states)


def solution(mesh):
    in_specs = (
        P(("seq", "tensor"), None),
        P(),
        P(None, None, "tensor"),
        P(None, None, "tensor"),
        P(None, "tensor"),
        P(None, "tensor"),
        P(None, None, "tensor"),
        P("tensor"),
        P(None, "tensor"),
        P("tensor"),
        P("tensor"),
        P("tensor"),
        P("tensor", None),
    )
    out_specs = (P(("seq", "tensor"), None), P(None, "tensor", None, None))
    return jax.shard_map(body, mesh=mesh, in_specs=in_specs, out_specs=out_specs, check_vma=False)
```

profile of v0, /device:TPU:0, one launch (start us, length us, event | category | flops | bytes accessed | tf_op | source)
XLA Modules:
  0.0 207.5 jit_solution(12037769887396977083)
XLA Ops:
  7.2 0.7 all-gather.7.cloned.1.call-update
  8.1 9.3 %copy.64 = bf16[512,8,2,512]{3,1,2,0:T(8,128)(2,1)} copy(bf16[512,8,2,512]{3,2,1,0:T(2,128)(2,1)} %bitcast.74) | data formatting | bytes 16777216
  18.5 0.6 fusion.52
  19.2 1.4 compare_and_fusion
  20.6 0.7 compare_convert_fusion.1
  21.4 32.9 %all-gather.7.cloned.1.call-done = bf16[256,4096]{1,0:T(8,128)(2,1)} async-done(((bf16[16,4096]{1,0:T(8,128)(2,1)}), bf16[256,4096]{1,0:T(8,128)(2,1)}) %all-gather.7.cloned.1.call-update) | async-done | bytes 2097168 | tf_op jit(solution)/shard_map/all_gather | solution.py:61
  54.3 6.5 %convolution_convert_fusion = bf16[256,1024]{1,0:T(8,128)(2,1)S(1)} fusion(bf16[256,4096]{1,0:T(8,128)(2,1)} %all-gather.7.cloned.1.call-done, bf16[4096,1024]{1,0:T(8,128)(2,1)} %bitcast.75), kind=kOutput, calls=%fused_computation.17 | convolution fusion | flops 2147745792 | bytes 11010048 | tf_op jit(solution)/shard_map/dot_general | solution.py:64
  60.9 0.8 convolution_convert_fusion.1
  61.7 3.4 %collective-permute-start = (bf16[3,640]{1,0:T(4,128)(2,1)S(1)}, bf16[3,640]{1,0:T(4,128)(2,1)S(1)}, u32[]{:S(2)}, u32[]{:S(2)}) collective-permute-start(bf16[3,640]{1,0:T(4,128)(2,1)S(1)} %pad_maximum_fusion.1), channel_id=1, source_target_pairs={{0,16},{1,17},{2,18},{3,19},{4,20},{5,21},{6,22},{7,23},{8,24},{9,... | collective-permute-start | bytes 11528 | tf_op jit(solution)/shard_map/ppermute | solution.py:18
  65.1 0.7 compare_select_fusion
  66.7 0.8 exponential_select_fusion
  68.5 0.7 multiply_bitcast_fusion
  70.0 2.7 %fusion.12 = f32[7,8,64,128]{3,2,0,1:T(8,128)S(1)} fusion(f32[256,8,7]{0,2,1:T(8,128)} %multiply_bitcast_fusion, f32[256,8,64]{0,2,1:T(8,128)S(1)} %convert.14, bf16[256,2,128]{2,0,1:T(8,128)(2,1)S(1)} %maximum_select_fusion), kind=kOutput, calls=%fused_computation.16 | convolution fusion | flops 1410203648 | bytes 2482176 | tf_op jit(solution)/shard_map/khs,shp,sn->khpn/dot_general | solution.py:131
  72.7 1.2 slice.104
  74.0 1.4 fusion.36
  75.5 1.2 slice_bitcast_fusion.1
  76.6 4.6 %all-gather.2 = f32[2,1,8]{2,1,0:T(1,128)} all-gather(f32[1,1,8]{2,1,0:T(1,128)} %slice_bitcast_fusion.1), channel_id=1, replica_groups=mesh['seq'=2,'tensor'=16] {'seq'}, dimensions={0}, use_global_device_ids=true | all-gather | bytes 96 | tf_op jit(solution)/shard_map/all_gather | solution.py:138
  81.2 1.9 convert_multiply_fusion
  83.2 2.1 copy.57
  85.3 15.0 %all_gather.17 = f32[2,8,64,128]{3,2,0,1:T(8,128)S(1)} all-gather(f32[1,8,64,128]{3,2,0,1:T(8,128)S(1)} %slice.102), channel_id=1, replica_groups=mesh['seq'=2,'tensor'=16] {'seq'}, dimensions={0}, use_global_device_ids=true | all-gather | bytes 786432 | tf_op jit(solution)/shard_map/all_gather | solution.py:139
  100.4 3.5 %fusion.15 = f32[256,8,64]{0,2,1:T(8,128)} fusion(bf16[256,8,64]{0,2,1:T(8,128)(2,1)S(1)} %bitcast.78, f32[8,256]{1,0:T(8,128)S(1)} %compare_select_fusion, f32[256,256]{1,0:T(8,128)S(1)} %fusion.39, f32[8,256]{1,0:T(8,128)} %copy-done.6, pred[256,256]{1,0:T(8,128)(4,1)} %fusion.36), kind=kOutput, calls=%fused_computation.18 | convolution fusion | flops 405274624 | bytes 1130496 | tf_op jit(solution)/shard_map/hts,shp->thp/dot_general | solution.py:108
  104.0 1.6 while.13
  104.0 0.7 fusion.68
  105.6 1.4 fusion.21
  107.0 5.4 %fusion.55 = f32[256,4096]{1,0:T(8,128)} fusion(bf16[256,512]{0,1:T(8,128)(2,1)S(1)} %bitcast.81, bf16[512,4096]{1,0:T(8,128)(2,1)} %param.27), kind=kOutput, calls=%fused_computation.103 | convolution fusion | flops 1073741824 | bytes 8650752 | tf_op jit(solution)/shard_map/dot_general | solution.py:162
  112.5 0.7 copy-done.10
  113.1 4.4 %all-gather.3 = f32[2,6,8]{2,1,0:T(8,128)S(1)} all-gather(f32[1,6,8]{2,1,0:T(8,128)S(1)} %slice_bitcast_fusion), channel_id=3, replica_groups=mesh['seq'=2,'tensor'=16] {'seq'}, dimensions={0}, use_global_device_ids=true | all-gather | bytes 576 | tf_op jit(solution)/shard_map/all_gather | solution.py:140
  117.6 5.5 %all-gather.9.cloned.1.call-done = f32[12,8,64,128]{3,2,0,1:T(8,128)} async-done(((f32[6,8,64,128]{3,2,0,1:T(8,128)}), f32[12,8,64,128]{3,2,0,1:T(8,128)}) %all-gather.9.cloned.1.call-update) | async-done | bytes 3145744 | tf_op jit(solution)/shard_map/all_gather | solution.py:141
  123.1 2.5 %add_reduce_fusion = f32[6,8,64,128]{3,2,0,1:T(8,128)S(1)} fusion(f32[2,6,8,64,128]{4,3,1,0,2:T(8,128)} %bitcast.76, f32[2,6,8]{1,0,2:T(2,128)S(1)} %copy.58, f32[2,8,64,128]{3,2,1,0:T(8,128)S(1)} %get-tuple-element.29), kind=kLoop, calls=%fused_computation.6 | loop fusion | flops 1966080 | bytes 5243264 | tf_op jit(solution)/shard_map/reduce_sum | solution.py:153
  125.6 1.3 copy.60
  127.0 72.4 %reduce-scatter.2.cloned.1.call-done = f32[16,4096]{1,0:T(8,128)} async-done(((f32[256,4096]{1,0:T(8,128)}), f32[16,4096]{1,0:T(8,128)}) %reduce-scatter.2.cloned.1.call-update) | async-done | bytes 262160 | tf_op jit(solution)/shard_map/reduce_scatter | solution.py:161
  199.4 1.6 convert_element_type.88
  (85 shorter events, 5.3 us)
Async XLA Ops:
  7.2 53.6 %copy-start = (bf16[4096,2,64]{0,2,1:T(8,128)(2,1)S(1)}, bf16[4096,2,64]{0,2,1:T(8,128)(2,1)}, u32[]{:S(2)}) copy-start(bf16[4096,2,64]{0,2,1:T(8,128)(2,1)} %param.18) | copy-start | bytes 3145732
  7.2 47.1 %all-gather.7.cloned.1.call-start = ((), (), s32[]{:S(2)}) async-start(), calls=%async_computation.1 | async-start | bytes 2228224 | tf_op jit(solution)/shard_map/all_gather | solution.py:61
  7.9 115.2 %all-gather.9.cloned.1.call-start = ((), (), s32[]{:S(2)}) async-start(), calls=%async_computation.3 | async-start | bytes 4718592 | tf_op jit(solution)/shard_map/all_gather | solution.py:141
  8.0 9.4 %copy-start.15 = (s32[6]{0:T(128)S(1)}, s32[6]{0:T(128)}, u32[]{:S(2)}) copy-start(s32[6]{0:T(128)} %param.16) | copy-start | bytes 76
  8.0 9.6 %copy-start.9 = (f32[4,2,64]{2,1,0:T(2,128)S(1)}, f32[4,2,64]{2,1,0:T(2,128)}, u32[]{:S(2)}) copy-start(f32[4,2,64]{2,1,0:T(2,128)} %param.21) | copy-start | bytes 6148
  8.0 9.7 %copy-start.14 = (f32[2,64]{1,0:T(2,128)S(1)}, f32[2,64]{1,0:T(2,128)}, u32[]{:S(2)}) copy-start(f32[2,64]{1,0:T(2,128)} %param.23) | copy-start | bytes 1540
  8.0 9.7 %copy-start.16 = (f32[8]{0:T(128)S(1)}, f32[8]{0:T(128)}, u32[]{:S(2)}) copy-start(f32[8]{0:T(128)} %param.25) | copy-start | bytes 100
  8.0 12.5 %copy-start.8 = (f32[4,512]{1,0:T(4,128)S(1)}, f32[4,512]{1,0:T(4,128)}, u32[]{:S(2)}) copy-start(f32[4,512]{1,0:T(4,128)} %param.20) | copy-start | bytes 24580
  8.1 12.5 %copy-start.11 = (f32[512]{0:T(512)S(1)}, f32[512]{0:T(512)}, u32[]{:S(2)}) copy-start(f32[512]{0:T(512)} %param.22) | copy-start | bytes 6148
  17.9 3.4 %copy-start.7 = (s32[256]{0:T(256)}, s32[256]{0:T(256)S(1)}, u32[]{:S(2)}) copy-start(s32[256]{0:T(256)S(1)} %get-tuple-element.76) | copy-start | bytes 3076
  54.3 6.5 %copy-start.1 = (bf16[256,4096]{1,0:T(8,128)(2,1)S(1)}, bf16[256,4096]{1,0:T(8,128)(2,1)}, u32[]{:S(2)}) copy-start(bf16[256,4096]{1,0:T(8,128)(2,1)} %all-gather.7.cloned.1.call-done) | copy-start | bytes 6291460
  60.8 6.7 %copy-start.2 = (bf16[256,1024]{1,0:T(8,128)(2,1)}, bf16[256,1024]{1,0:T(8,128)(2,1)S(1)}, u32[]{:S(2)}) copy-start(bf16[256,1024]{1,0:T(8,128)(2,1)S(1)} %convolution_convert_fusion) | copy-start | bytes 1572868
  60.8 4.2 %copy-start.5 = (bf16[4096,8]{0,1:T(8,128)(2,1)S(1)}, bf16[4096,8]{0,1:T(8,128)(2,1)}, u32[]{:S(2)}) copy-start(bf16[4096,8]{0,1:T(8,128)(2,1)} %param.19) | copy-start | bytes 196612
  60.8 4.2 %copy-start.12 = (f32[8]{0:T(128)S(1)}, f32[8]{0:T(128)}, u32[]{:S(2)}) copy-start(f32[8]{0:T(128)} %param.24) | copy-start | bytes 100
  61.7 5.9 %collective-permute-start = (bf16[3,640]{1,0:T(4,128)(2,1)S(1)}, bf16[3,640]{1,0:T(4,128)(2,1)S(1)}, u32[]{:S(2)}, u32[]{:S(2)}) collective-permute-start(bf16[3,640]{1,0:T(4,128)(2,1)S(1)} %pad_maximum_fusion.1), channel_id=1, source_target_pairs={{0,16},{1,17},{2,18},{3,19},{4,20},{5,21},{6,22},{7,23},{8,24},{9,... | collective-permute-start | bytes 11528 | tf_op jit(solution)/shard_map/ppermute | solution.py:18
  66.7 3.2 %copy-start.6 = (f32[8,256]{1,0:T(8,128)}, f32[8,256]{1,0:T(8,128)S(1)}, u32[]{:S(2)}) copy-start(f32[8,256]{1,0:T(8,128)S(1)} %get-tuple-element.93) | copy-start | bytes 24580
  68.5 1.4 collective-permute-start.1
  74.0 125.4 %reduce-scatter.2.cloned.1.call-start = ((), (), s32[]{:S(2)}) async-start(), calls=%async_computation.2 | async-start | bytes 4456448 | tf_op jit(solution)/shard_map/reduce_scatter | solution.py:161
  100.4 3.5 %copy-start.4 = (f32[2,8,64,128]{3,2,1,0:T(8,128)S(1)}, f32[2,8,64,128]{3,2,1,0:T(8,128)}, u32[]{:S(2)}) copy-start(f32[2,8,64,128]{3,2,1,0:T(8,128)} %custom-call.2) | copy-start | bytes 1572868
  104.0 1.6 copy-start.3
  104.0 1.6 copy-start.13
  112.4 0.7 copy-start.10
Sparse Core Ops, SparseCore 0:
  10.2 44.0 all-gather.6
  74.1 48.9 all-gather.8
  127.0 72.3 reduce-scatter.1
where the time goes:
time: 208 us
  waiting for transfers between devices  112 us (54%)
  blocking collectives  24 us (12%)
  matrix products  22 us (11%)
  local copies, waits for them, and re-layouts  18.7 us (9%)
  between operations  14.1 us (7%)
  other arithmetic  13.1 us (6%)
  starting transfers between devices  3.56 us (2%)
    reduce_scatter x1, waiting for transfers between devices, body(): lax.psum_scatter(jnp.dot(gated, proj_out, preferred_element_type=jnp.floa...  72.4 us
    all_gather x1, waiting for transfers between devices, body(): piece = lax.all_gather(tokens, 'tensor', axis=0, tiled=True)  32.9 us
    all_gather x1, blocking collectives, body(): lax.all_gather(shard_state[None], 'seq', axis=0, tiled=True)  15 us
    unnamed x39, local copies, waits for them, and re-layouts  12.6 us
    dot_general x1, matrix products, body(): jnp.dot(piece, zx_flat, preferred_element_type=jnp.float32)  6.49 us
    all_gather x1, waiting for transfers between devices, body(): lax.all_gather(end_local[None], 'seq', axis=0, tiled=True)  5.54 us
    dot_general x1, matrix products, body(): jnp.dot(gated, proj_out, preferred_element_type=jnp.float32)  5.4 us
    all_gather x1, blocking collectives, body(): lax.all_gather(shard_gain[None], 'seq', axis=0, tiled=True)  4.62 us
  transfers between devices with their start and end apart: 5, of which 4 were waited for; matrix products, arithmetic and copies ran while one was open for 19% of the time, Pallas kernels for 0%

commit v1 on v0

--- a/solution.py
+++ b/solution.py
@@ -4,6 +4,19 @@
 from jax.sharding import PartitionSpec as P
 
 GROUPS = 8
+
+
+def _group_paths(on_dim, base_x):
+    vec_out, t1, near = (jax.lax.axis_size("seq"), jax.lax.axis_index("seq"), base_x.shape[on_dim])
+    x_new, z2 = (base_x, 1)
+    while z2 < vec_out:
+        leaves = []
+        for tick in range(vec_out):
+            leaves.append((tick, (tick - z2) % vec_out))
+        x_new = jnp.concatenate([x_new, jax.lax.ppermute(x_new, "seq", leaves)], axis=on_dim)
+        z2 = 2 * z2
+    view_out = jnp.roll(x_new, t1 * near, axis=on_dim)
+    return view_out
 
 
 def partner_2(value, axis, bit):
@@ -138,7 +151,7 @@
         lax.all_gather(shard_gain[None], "seq", axis=0, tiled=True),
         lax.all_gather(shard_state[None], "seq", axis=0, tiled=True),
         lax.all_gather(end_gain_seg[None], "seq", axis=0, tiled=True),
-        lax.all_gather(end_local[None], "seq", axis=0, tiled=True),
+        _group_paths(0, end_local[None]),
     )
     gains_all, states_all, egains_all, elocal_all = gathered
 

time: 208 us -> 180 us (0.87)
  waiting for transfers between devices: 112 us -> 63.2 us
  blocking collectives: 24 us -> 47.2 us
  matrix products: 22 us -> 19.4 us
  local copies, waits for them, and re-layouts: 18.7 us -> 16.5 us
    reduce_scatter x1, waiting for transfers between devices: 72.4 us -> 30.3 us  [body(): lax.psum_scatter(jnp.dot(gated, proj_out, preferred_element_type=jnp.floa...]
    all_gather x1, blocking collectives: 4.38 us -> 34.3 us  [body(): lax.all_gather(end_gain_seg[None], 'seq', axis=0, tiled=True)]
    all_gather x1, blocking collectives: 15 us -> 8.67 us  [body(): lax.all_gather(shard_state[None], 'seq', axis=0, tiled=True)]
    all_gather x1 -> x0, waiting for transfers between devices: 5.54 us -> none  [body(): lax.all_gather(end_local[None], 'seq', axis=0, tiled=True)]
    dot_general x1, matrix products: 5.4 us -> 3.24 us  [body(): jnp.dot(gated, proj_out, preferred_element_type=jnp.float32)]
    unnamed x39 -> x35, local copies, waits for them, and re-layouts: 12.6 us -> 11.4 us
  transfers between devices with their start and end apart: 5 -> 5, of which waited for: 4 -> 2; matrix products, arithmetic and copies ran while one was open for 19% -> 13% of each run, Pallas kernels for 0% -> 0%
where the time goes in v1:
time: 180 us; the launch traced here: 179 us
  waiting for transfers between devices  63.2 us (35%)
  blocking collectives  47.2 us (26%)
  matrix products  19.4 us (11%)
  local copies, waits for them, and re-layouts  16.5 us (9%)
  between operations  14.4 us (8%)
  other arithmetic  14.1 us (8%)
  starting transfers between devices  4.42 us (2%)
    all_gather x1, blocking collectives, body(): lax.all_gather(end_gain_seg[None], 'seq', axis=0, tiled=True)  34.3 us
    all_gather x1, waiting for transfers between devices, body(): piece = lax.all_gather(tokens, 'tensor', axis=0, tiled=True)  32.2 us
    reduce_scatter x1, waiting for transfers between devices, body(): lax.psum_scatter(jnp.dot(gated, proj_out, preferred_element_type=jnp.floa...  30.3 us
    unnamed x35, local copies, waits for them, and re-layouts  11.4 us
    all_gather x1, blocking collectives, body(): lax.all_gather(shard_state[None], 'seq', axis=0, tiled=True)  8.67 us
    dot_general x1, matrix products, body(): jnp.dot(piece, zx_flat, preferred_element_type=jnp.float32)  6.49 us
    all_gather x1, blocking collectives, body(): lax.all_gather(shard_gain[None], 'seq', axis=0, tiled=True)  4.16 us
  transfers between devices with their start and end apart: 5, of which 2 were waited for; matrix products, arithmetic and copies ran while one was open for 13% of the time, Pallas kernels for 0%

profile of v1, /device:TPU:0, one launch (start us, length us, event | category | flops | bytes accessed | tf_op | source)
XLA Modules:
  0.0 179.1 jit_solution(15415721590930744377)
XLA Ops:
  7.2 0.7 all-gather.5.cloned.1.call-update
  8.1 9.3 %copy.60 = bf16[512,8,2,512]{3,1,2,0:T(8,128)(2,1)} copy(bf16[512,8,2,512]{3,2,1,0:T(2,128)(2,1)} %bitcast.75) | data formatting | bytes 16777216
  19.2 1.4 compare_and_fusion
  21.3 0.7 fusion.41
  22.1 32.2 %all-gather.5.cloned.1.call-done = bf16[256,4096]{1,0:T(8,128)(2,1)} async-done(((bf16[16,4096]{1,0:T(8,128)(2,1)}), bf16[256,4096]{1,0:T(8,128)(2,1)}) %all-gather.5.cloned.1.call-update) | async-done | bytes 2097168 | tf_op jit(solution)/shard_map/all_gather | solution.py:74
  54.3 6.5 %convolution_convert_fusion = bf16[256,1024]{1,0:T(8,128)(2,1)S(1)} fusion(bf16[256,4096]{1,0:T(8,128)(2,1)} %all-gather.5.cloned.1.call-done, bf16[4096,1024]{1,0:T(8,128)(2,1)} %bitcast.76), kind=kOutput, calls=%fused_computation.26 | convolution fusion | flops 2147745792 | bytes 11010048 | tf_op jit(solution)/shard_map/dot_general | solution.py:77
  61.0 0.8 convolution_convert_fusion.1
  61.8 3.4 %collective-permute-start = (bf16[3,640]{1,0:T(4,128)(2,1)S(1)}, bf16[3,640]{1,0:T(4,128)(2,1)S(1)}, u32[]{:S(2)}, u32[]{:S(2)}) collective-permute-start(bf16[3,640]{1,0:T(4,128)(2,1)S(1)} %pad_maximum_fusion.1), channel_id=1, source_target_pairs={{0,16},{1,17},{2,18},{3,19},{4,20},{5,21},{6,22},{7,23},{8,24},{9,... | collective-permute-start | bytes 11528 | tf_op jit(solution)/shard_map/ppermute | solution.py:31
  65.2 0.7 compare_select_fusion
  68.7 0.7 multiply_bitcast_fusion
  69.4 4.2 %all-gather.1 = f32[2,1,8]{2,1,0:T(1,128)} all-gather(f32[1,1,8]{2,1,0:T(1,128)S(1)} %slice_bitcast_fusion.2), channel_id=1, replica_groups=mesh['seq'=2,'tensor'=16] {'seq'}, dimensions={0}, use_global_device_ids=true | all-gather | bytes 96 | tf_op jit(solution)/shard_map/all_gather | solution.py:151
  73.5 1.0 copy.54
  74.9 0.9 fusion.44
  75.8 2.7 %fusion.17 = f32[7,8,64,128]{3,2,0,1:T(8,128)S(1)} fusion(f32[256,8,7]{0,2,1:T(8,128)} %multiply_bitcast_fusion, f32[256,8,64]{0,2,1:T(8,128)S(1)} %convert.14, bf16[256,2,128]{2,0,1:T(8,128)(2,1)S(1)} %maximum_select_fusion), kind=kOutput, calls=%fused_computation.25 | convolution fusion | flops 1410203648 | bytes 2482176 | tf_op jit(solution)/shard_map/khs,shp,sn->khpn/dot_general | solution.py:144
  78.5 8.7 %all_gather.14 = f32[2,8,64,128]{3,2,0,1:T(8,128)} all-gather(f32[1,8,64,128]{3,2,0,1:T(8,128)S(1)} %slice.102), channel_id=1, replica_groups=mesh['seq'=2,'tensor'=16] {'seq'}, dimensions={0}, use_global_device_ids=true | all-gather | bytes 786432 | tf_op jit(solution)/shard_map/all_gather | solution.py:152
  87.2 4.9 %while.13 = (s32[]{:T(128)}, f32[8,64,128]{2,1,0:T(8,128)S(1)}, f32[2,8,64,128]{3,2,1,0:T(8,128)}, f32[2,8]{1,0:T(2,128)}, f32[2,8,64,128]{3,2,0,1:T(8,128)}, /*index=5*/s32[]{:T(128)}, s32[]{:T(128)}) while((s32[]{:T(128)}, f32[8,64,128]{2,1,0:T(8,128)S(1)}, f32[2,8,64,128]{3,2,1,0:T(8,128)}, f32[2,8]{1,0:T(2,128)}, ...), condition=%wide.region_7.8_spmd.clone, body=%wide.region_6.7_spmd.clone.sunk | while | flops 262147 | bytes 1310924 | solution.py:162
  87.2 0.7 bitcast_dynamic-update-slice_fusion.2
  87.9 0.7 fusion.72
  88.6 1.0 bitcast_add_fusion.2
  89.7 0.7 bitcast_dynamic-update-slice_fusion.2
  90.4 0.7 fusion.72
  91.1 1.0 bitcast_add_fusion.2
  92.1 2.9 %fusion.20 = f32[256,8,64]{0,2,1:T(8,128)S(1)} fusion(bf16[256,8,64]{0,2,1:T(8,128)(2,1)S(1)} %bitcast.78, f32[8,256]{1,0:T(8,128)S(1)} %compare_select_fusion, f32[256,256]{1,0:T(8,128)} %fusion.44, f32[8,256]{1,0:T(8,128)} %copy-done.4, pred[256,256]{1,0:T(8,128)(4,1)} %fusion.41), kind=kOutput, calls=%fused_computation.27 | convolution fusion | flops 405274624 | bytes 1130496 | tf_op jit(solution)/shard_map/hts,shp->thp/dot_general | solution.py:121
  95.1 1.5 fusion.26
  96.6 3.2 %fusion.60 = f32[256,4096]{1,0:T(8,128)} fusion(bf16[256,512]{0,1:T(8,128)(2,1)S(1)} %bitcast.81, bf16[512,4096]{1,0:T(8,128)(2,1)S(1)} %copy-done.1), kind=kOutput, calls=%fused_computation.112 | convolution fusion | flops 1073741824 | bytes 8650752 | tf_op jit(solution)/shard_map/dot_general | solution.py:175
  99.9 1.2 slice_bitcast_fusion
  101.1 0.9 collective-permute-start.2
  102.0 34.3 %all-gather.2 = f32[2,6,8]{2,1,0:T(8,128)S(1)} all-gather(f32[1,6,8]{2,1,0:T(8,128)S(1)} %slice_bitcast_fusion.1), channel_id=2, replica_groups=mesh['seq'=2,'tensor'=16] {'seq'}, dimensions={0}, use_global_device_ids=true | all-gather | bytes 576 | tf_op jit(solution)/shard_map/all_gather | solution.py:153
  136.4 2.6 %fusion.7 = f32[6,8,64,128]{3,2,0,1:T(8,128)S(1)} fusion(s32[]{:T(128)S(6)} %select_n.73, f32[1,6,8,64,128]{4,3,1,2,0:T(8,128)} %slice_bitcast_fusion, f32[1,6,8,64,128]{4,3,1,2,0:T(8,128)S(1)} %collective-permute-done.2, f32[2,6,8]{1,2,0:T(8,128)S(1)} %copy.55, f32[2,8,64,128]{3,2,1,0:T(8,128)} %get-tuple-element.29), kind=kLoop, calls=%fused_computation.14 | loop fusion | flops 4325376 | bytes 5243268 | tf_op jit(solution)/shard_map/reduce_sum | solution.py:166
  139.1 1.3 copy.56
  140.4 30.3 %reduce-scatter.2.cloned.1.call-done = f32[16,4096]{1,0:T(8,128)} async-done(((f32[256,4096]{1,0:T(8,128)}), f32[16,4096]{1,0:T(8,128)}) %reduce-scatter.2.cloned.1.call-update) | async-done | bytes 262160 | tf_op jit(solution)/shard_map/reduce_scatter | solution.py:174
  170.7 1.6 convert_element_type.88
  (80 shorter events, 6.1 us)
Async XLA Ops:
  7.2 53.8 %copy-start = (bf16[4096,2,64]{0,2,1:T(8,128)(2,1)S(1)}, bf16[4096,2,64]{0,2,1:T(8,128)(2,1)}, u32[]{:S(2)}) copy-start(bf16[4096,2,64]{0,2,1:T(8,128)(2,1)} %param.18) | copy-start | bytes 3145732
  7.2 47.1 %all-gather.5.cloned.1.call-start = ((), (), s32[]{:S(2)}) async-start(), calls=%async_computation.1 | async-start | bytes 2228224 | tf_op jit(solution)/shard_map/all_gather | solution.py:74
  7.9 162.8 %reduce-scatter.2.cloned.1.call-start = ((), (), s32[]{:S(2)}) async-start(), calls=%async_computation.2 | async-start | bytes 4456448 | tf_op jit(solution)/shard_map/reduce_scatter | solution.py:174
  8.0 9.4 %copy-start.13 = (s32[6]{0:T(128)S(1)}, s32[6]{0:T(128)}, u32[]{:S(2)}) copy-start(s32[6]{0:T(128)} %param.16) | copy-start | bytes 76
  8.0 9.6 %copy-start.6 = (f32[4,2,64]{2,1,0:T(2,128)S(1)}, f32[4,2,64]{2,1,0:T(2,128)}, u32[]{:S(2)}) copy-start(f32[4,2,64]{2,1,0:T(2,128)} %param.21) | copy-start | bytes 6148
  8.0 9.7 %copy-start.12 = (f32[2,64]{1,0:T(2,128)S(1)}, f32[2,64]{1,0:T(2,128)}, u32[]{:S(2)}) copy-start(f32[2,64]{1,0:T(2,128)} %param.23) | copy-start | bytes 1540
  8.0 9.7 %copy-start.14 = (f32[8]{0:T(128)S(1)}, f32[8]{0:T(128)}, u32[]{:S(2)}) copy-start(f32[8]{0:T(128)} %param.25) | copy-start | bytes 100
  8.0 12.5 %copy-start.5 = (f32[4,512]{1,0:T(4,128)S(1)}, f32[4,512]{1,0:T(4,128)}, u32[]{:S(2)}) copy-start(f32[4,512]{1,0:T(4,128)} %param.20) | copy-start | bytes 24580
  8.1 12.5 %copy-start.9 = (f32[512]{0:T(512)S(1)}, f32[512]{0:T(512)}, u32[]{:S(2)}) copy-start(f32[512]{0:T(512)} %param.22) | copy-start | bytes 6148
  54.3 6.7 %copy-start.2 = (bf16[256,4096]{1,0:T(8,128)(2,1)S(1)}, bf16[256,4096]{1,0:T(8,128)(2,1)}, u32[]{:S(2)}) copy-start(bf16[256,4096]{1,0:T(8,128)(2,1)} %all-gather.5.cloned.1.call-done) | copy-start | bytes 6291460
  61.0 4.2 %copy-start.3 = (bf16[4096,8]{0,1:T(8,128)(2,1)S(1)}, bf16[4096,8]{0,1:T(8,128)(2,1)}, u32[]{:S(2)}) copy-start(bf16[4096,8]{0,1:T(8,128)(2,1)} %param.19) | copy-start | bytes 196612
  61.0 4.2 %copy-start.10 = (f32[8]{0:T(128)S(1)}, f32[8]{0:T(128)}, u32[]{:S(2)}) copy-start(f32[8]{0:T(128)} %param.24) | copy-start | bytes 100
  61.8 5.9 %collective-permute-start = (bf16[3,640]{1,0:T(4,128)(2,1)S(1)}, bf16[3,640]{1,0:T(4,128)(2,1)S(1)}, u32[]{:S(2)}, u32[]{:S(2)}) collective-permute-start(bf16[3,640]{1,0:T(4,128)(2,1)S(1)} %pad_maximum_fusion.1), channel_id=1, source_target_pairs={{0,16},{1,17},{2,18},{3,19},{4,20},{5,21},{6,22},{7,23},{8,24},{9,... | collective-permute-start | bytes 11528 | tf_op jit(solution)/shard_map/ppermute | solution.py:31
  66.8 7.9 %copy-start.4 = (f32[8,256]{1,0:T(8,128)}, f32[8,256]{1,0:T(8,128)S(1)}, u32[]{:S(2)}) copy-start(f32[8,256]{1,0:T(8,128)S(1)} %get-tuple-element.93) | copy-start | bytes 24580
  67.0 0.6 copy-start.7
  68.6 6.2 %collective-permute-start.1 = (bf16[256,2,64]{2,0,1:T(8,128)(2,1)S(1)}, bf16[256,2,64]{2,0,1:T(8,128)(2,1)S(1)}, u32[]{:S(2)}, u32[]{:S(2)}) collective-permute-start(bf16[256,2,64]{2,0,1:T(8,128)(2,1)S(1)} %copy.50), channel_id=1, source_target_pairs={{0,1},{1,0},{2,3},{3,2},{4,5},{5,4},{6,7},{7,6},{8,9},{9,8},{10,11... | collective-permute-start | bytes 196616 | tf_op jit(solution)/shard_map/ppermute | solution.py:25
  92.1 2.9 %copy-start.11 = (f32[8]{0:T(128)S(1)}, f32[8]{0:T(128)}, u32[]{:S(2)}) copy-start(f32[8]{0:T(128)} %param.26) | copy-start | bytes 100
  92.1 4.5 %copy-start.1 = (bf16[512,4096]{1,0:T(8,128)(2,1)S(1)}, bf16[512,4096]{1,0:T(8,128)(2,1)}, u32[]{:S(2)}) copy-start(bf16[512,4096]{1,0:T(8,128)(2,1)} %param.27) | copy-start | bytes 12582916
  99.9 2.2 %copy-start.8 = (f32[7,8]{1,0:T(8,128)S(1)}, f32[7,8]{1,0:T(8,128)}, u32[]{:S(2)}) copy-start(f32[7,8]{1,0:T(8,128)} %copy-done.7) | copy-start | bytes 676
  101.1 35.3 %collective-permute-start.2 = (f32[1,6,8,64,128]{4,3,1,2,0:T(8,128)}, f32[1,6,8,64,128]{4,3,1,2,0:T(8,128)S(1)}, u32[]{:S(2)}, u32[]{:S(2)}) collective-permute-start(f32[1,6,8,64,128]{4,3,1,2,0:T(8,128)} %slice_bitcast_fusion), channel_id=1, source_target_pairs={{0,16},{16,0},{1,17},{17,1},{2,18},{18,2},{3,19},{19,3},{4,20},{20... | collective-permute-start | bytes 4718600 | tf_op jit(solution)/shard_map/ppermute | solution.py:16
Sparse Core Ops, SparseCore 0:
  10.2 44.0 all-gather.4
  100.0 70.6 reduce-scatter.1
